TPU v7x, 32 devices: a whole 2x2x4 slice. The times are simulated.
32 devices in a mesh: dp: 4 (over x, core), tm: 8 (over z, y).
Axes of the slice: x: 2, y: 2, z: 4, core: 2. Of those that a mesh axis runs over, the one named last changes fastest.
Arguments:
- latent: float32 [4, 64, 4096], P('dp', None, 'tm'), may hold values from -40 to 40
- target: float32 [4, 8192], P('dp', 'tm'), may hold values from -20 to 20
- up_kernel: float32 [4, 32, 64], replicated, may hold values from -0.5 to 0.5
- inner_kernel: float32 [3, 16, 32], replicated, may hold values from -0.625 to 0.625
- outer_kernel: float32 [32, 16], replicated, may hold values from -1.5 to 1.5
- out_kernel: float32 [7, 32], replicated, may hold values from -0.375 to 0.375
Outputs:
- latent_grad: float32 [4, 64, 4096], P('dp', None, 'tm')
- up_update: float32 [4, 32, 64], replicated
- inner_update: float32 [3, 16, 32], replicated
- outer_update: float32 [32, 16], replicated
- out_update: float32 [7, 32], replicated
All inputs are finite; a program needn't handle non-finite values.
Results may differ from a plain program's by a relative error of at most 0.0003.
Values sent between devices are 32-bit elements; how exact they have to be, the bound alone decides.
No kernel may reach another device: no remote copies, remote signals or barrier semaphores. Data moves between devices by JAX's collectives and lax.ppermute only.
A program may use at most 64 MiB of HBM per device.

v0:
```python
import jax
import jax.numpy as jnp
from jax import lax
from jax.sharding import PartitionSpec as P

MELS = 64
WIN_COARSE = 1024
WIN_FINE = 256
LOSS_WEIGHTS = (0.25, 0.5, 0.5)


def padded_2(cells, sides, width):
    for axis, dim in sides:
        count = lax.axis_size(axis)
        ends = count - 1
        head = lax.slice_in_dim(cells, 0, width, axis=dim)
        tail = lax.slice_in_dim(cells, cells.shape[dim] - width, cells.shape[dim], axis=dim)
        cells = jnp.concatenate(
            [
                lax.ppermute(tail, axis, [(i, (i + 1) % count) for i in range(ends)]),
                cells,
                lax.ppermute(head, axis, [((i + 1) % count, i) for i in range(ends)]),
            ],
            axis=dim,
        )
    return cells


def from_behind(x, axis, by):
    peers = lax.axis_size(axis)
    pairs = [(i, i + by) for i in range(peers) if 0 <= i + by < peers]
    return lax.ppermute(x, axis, pairs)


def product(form, left, right):
    return jnp.einsum(
        form, left, right, precision=lax.Precision.HIGHEST, preferred_element_type=jnp.float32
    )


def mel_bank(window, mel_count):
    half_window = window // 2
    top_mel = 2595.0 * jnp.log10(1.0 + 12000.0 / 700.0)
    points = (jnp.arange(mel_count + 1, dtype=jnp.float32) + 1.0) / (mel_count + 2.0) * top_mel
    centers = 700.0 * (jnp.power(10.0, points / 2595.0) - 1.0) / 12000.0 * half_window
    spacing = jnp.maximum(centers[1:] - centers[:-1], 1.0)
    places = jnp.arange(half_window, dtype=jnp.float32)[:, None]
    return jnp.maximum(0.0, 1.0 - jnp.abs(places - centers[None, :mel_count]) / spacing[None, :])


def dft_table(window):
    half_window = window // 2
    sample = jnp.arange(window, dtype=jnp.int32)[:, None]
    freq_index = jnp.arange(half_window, dtype=jnp.int32)[None, :]
    angles = (sample * freq_index % window).astype(jnp.float32) * (2.0 * jnp.pi / window)
    hann_taper = 0.5 - 0.5 * jnp.cos(sample.astype(jnp.float32) * (2.0 * jnp.pi / window))
    return jnp.concatenate([hann_taper * jnp.cos(angles), -hann_taper * jnp.sin(angles)], axis=1)


def framed(signal, window, frame_count):
    hop_size = window // 4
    blocks = signal.reshape(signal.shape[:-1] + (frame_count + 3, hop_size))
    return jnp.concatenate(
        [blocks[..., offset : offset + frame_count, :] for offset in range(4)], axis=-1
    )


def mel_energy(signal, window, frame_count):
    frames = framed(signal, window, frame_count)
    spectra = product("...nf,fk->...nk", frames, dft_table(window))
    half_window = window // 2
    energy = spectra[..., :half_window] ** 2 + spectra[..., half_window:] ** 2
    return product("...nk,km->...nm", energy, mel_bank(window, MELS))


def spectral_loss(signal, target_mel, window, frame_count):
    level = jnp.sqrt(mel_energy(signal, window, frame_count) + 1.0)
    return jnp.sum((level - jnp.sqrt(target_mel + 1.0)) ** 2)


def elu_slope(values):
    return jnp.where(values > 0, 1.0, jnp.exp(jnp.minimum(values, 0.0)))


def apply_mask(values, mask):
    return values * mask


def upsample_forward(values, kernel, stride, previous):
    lagged = jnp.concatenate([previous, values[:, :, :-1]], axis=2)
    phases = product("pij,bjm->bimp", kernel[:stride], values) + product(
        "pij,bjm->bimp", kernel[stride:], lagged
    )
    return (phases.reshape(phases.shape[0], phases.shape[1], -1), lagged)


def taps_forward(padded, kernel, length):
    summed = product("oi,bil->bol", kernel[0], padded[:, :, :length])
    for offset in range(1, kernel.shape[0]):
        summed = summed + product(
            "oi,bil->bol", kernel[offset], padded[:, :, offset : offset + length]
        )
    return summed


def decode_forward(activated, weights, movers, clip_mask):
    up_kernel, inner_kernel, outer_kernel, out_kernel = weights
    lend_frame, border_inner, border_output = movers
    upper, lagged = upsample_forward(activated, up_kernel, 2, lend_frame(activated[:, :, -1:]))
    upper = apply_mask(upper, clip_mask)
    padded_inner = border_inner(jax.nn.elu(upper))
    inner_out = taps_forward(padded_inner, inner_kernel, upper.shape[2])
    hidden = jax.nn.elu(inner_out)
    mixed = apply_mask(upper + product("oi,bil->bol", outer_kernel, hidden), clip_mask)
    padded_output = border_output(jax.nn.elu(mixed))
    waveform = taps_forward(padded_output, out_kernel[:, None, :], upper.shape[2])[:, 0, :]
    return (waveform, (upper, lagged, padded_inner, inner_out, hidden, mixed, padded_output))


def taps_backward(grad_out, padded, kernel, length, keep):
    tap_count = kernel.shape[0]
    row_grad = apply_mask(grad_out, keep)
    kernel_rows = jnp.stack(
        [
            product("nbol,bil->nboi", row_grad, padded[:, :, offset : offset + length])
            for offset in range(tap_count)
        ],
        axis=2,
    )
    spread = jnp.zeros(grad_out.shape[:2] + (kernel.shape[2], length + tap_count - 1), jnp.float32)
    for offset in range(tap_count):
        moved = product("oi,nbol->nbil", kernel[offset], grad_out)
        spread = spread + jnp.pad(moved, ((0, 0), (0, 0), (0, 0), (offset, tap_count - 1 - offset)))
    return (kernel_rows, spread)


def rims_backward(spread, rim_width):
    interior = spread[..., rim_width:-rim_width]
    return interior


def residual_backward(
    grad_mixed, upper, padded, inner_out, hidden, inner_kernel, outer_kernel, keep
):
    length = upper.shape[-1]
    outer_rows = product("nbol,bil->nboi", apply_mask(grad_mixed, keep), hidden)
    grad_inner = product("oi,nbol->nbil", outer_kernel, grad_mixed) * elu_slope(inner_out)
    inner_rows, spread = taps_backward(grad_inner, padded, inner_kernel, length, keep)
    grad_rectified = rims_backward(spread, 1)
    return (grad_mixed + grad_rectified * elu_slope(upper), inner_rows, outer_rows)


def upsample_backward(grad_upper, values, lagged, kernel, stride, keep):
    phase_shape = grad_upper.shape[:3] + (values.shape[-1], stride)
    grad_phase = grad_upper.reshape(phase_shape)
    row_phase = apply_mask(grad_upper, keep).reshape(phase_shape)
    first_rows = product("nbimp,bjm->nbpij", row_phase, values)
    second_rows = product("nbimp,bjm->nbpij", row_phase, lagged)
    grad_values = product("pij,nbimp->nbjm", kernel[:stride], grad_phase)
    grad_lagged = product("pij,nbimp->nbjm", kernel[stride:], grad_phase)
    arrived = jnp.zeros_like(grad_lagged[..., :1])
    grad_values = grad_values + jnp.concatenate([grad_lagged[..., 1:], arrived], axis=-1)
    return (grad_values, jnp.concatenate([first_rows, second_rows], axis=2))


def local(latent, target, up_kernel, inner_kernel, outer_kernel, out_kernel):
    weights = (up_kernel, inner_kernel, outer_kernel, out_kernel)
    clips_here = target.shape[0]
    samples = target.shape[1]
    frames_here = latent.shape[2]
    latent_in = padded_2(latent, (("tm", 2),), 4)
    start_frame = 4
    margin = 8

    def lend_frame(edge):
        return jnp.zeros_like(edge)

    def border_inner(values):
        return jnp.pad(values, ((0, 0), (0, 0), (1, 1)))

    def border_output(values):
        return jnp.pad(values, ((0, 0), (0, 0), (3, 3)))

    shard_index = lax.axis_index("tm")
    shard_total = lax.axis_size("tm")
    wide_length = samples + 2 * margin
    local_places = jnp.arange(wide_length, dtype=jnp.int32)
    clip_places = samples * shard_index - margin + local_places
    clip_mask = ((clip_places >= 0) & (clip_places < samples * shard_total)).astype(jnp.float32)
    keep_rows = ((local_places >= margin) & (local_places < margin + samples)).astype(jnp.float32)
    activated = jax.nn.elu(latent_in)
    wave_all, saved = decode_forward(
        activated, weights, (lend_frame, border_inner, border_output), clip_mask
    )
    upper, lagged, padded_inner, inner_out, hidden, mixed, padded_output = saved
    waveform = wave_all[:, margin : margin + samples]
    tail_length = 3 * WIN_COARSE // 4
    wave_next, target_next = from_behind(
        (waveform[:, :tail_length], target[:, :tail_length]), "tm", -1
    )
    long_wave = jnp.concatenate([waveform, wave_next], axis=1)
    long_target = jnp.concatenate([target, target_next], axis=1)
    gradients = [2.0 * (waveform - target)]
    tails = []
    for window in (WIN_COARSE, WIN_FINE):
        hop_size = window // 4
        frame_count = samples // hop_size
        span = samples + 3 * hop_size
        target_mel = mel_energy(long_target[:, :span], window, frame_count)

        def scale_loss(signal):
            return spectral_loss(signal, target_mel, window, frame_count)

        local_grad = jax.grad(scale_loss)(long_wave[:, :span])
        gradients.append(local_grad[:, :samples])
        tails.append(jnp.pad(local_grad[:, samples:], ((0, 0), (0, tail_length - 3 * hop_size))))
    coarse_in, fine_in = from_behind((tails[0], tails[1]), "tm", 1)
    gradients[1] = gradients[1] + jnp.pad(coarse_in, ((0, 0), (0, samples - tail_length)))
    gradients[2] = gradients[2] + jnp.pad(fine_in, ((0, 0), (0, samples - tail_length)))
    squares = jnp.stack([jnp.sum(member * member, axis=1) for member in gradients], axis=1)
    squares = lax.psum(squares, "tm")
    total_samples = samples * lax.axis_size("tm")
    grad_scale = jnp.asarray(LOSS_WEIGHTS, jnp.float32)[None, :] / jnp.sqrt(
        squares / total_samples + 1e-06
    )
    streams = (
        gradients[0] * grad_scale[:, 0, None]
        + gradients[1] * grad_scale[:, 1, None]
        + gradients[2] * grad_scale[:, 2, None]
    )[None]
    row_weights = jnp.ones((1, clips_here), jnp.float32)
    streams_wide = padded_2(streams, (("tm", 2),), 8)
    wave_length = mixed.shape[2]
    out_taps = out_kernel[:, None, :]
    kernel_rows_out, spread_out = taps_backward(
        streams_wide[:, :, None, :], padded_output, out_taps, wave_length, keep_rows
    )
    out_rows = kernel_rows_out[:, :, :, 0, :]
    grad_final = rims_backward(spread_out, 3)
    grad_mixed = apply_mask(grad_final * elu_slope(mixed), clip_mask)
    grad_upper, inner_rows, outer_rows = residual_backward(
        grad_mixed, upper, padded_inner, inner_out, hidden, inner_kernel, outer_kernel, keep_rows
    )
    grad_activated, up_rows = upsample_backward(
        apply_mask(grad_upper, clip_mask), activated, lagged, up_kernel, 2, keep_rows
    )
    grad_latent_rows = grad_activated[..., start_frame : start_frame + frames_here] * elu_slope(
        latent
    )
    latent_grad = product("nb,nbcm->bcm", row_weights, grad_latent_rows)
    local_totals = [
        product("nb,nb...->...", row_weights, member)
        for member in (up_rows, inner_rows, outer_rows, out_rows)
    ]
    param_count = sum((member.size for member in local_totals))
    summed = lax.psum(
        (local_totals[0], local_totals[1], local_totals[2], local_totals[3]), ("dp", "tm")
    )
    squares_all = sum((jnp.sum(member * member) for member in summed))
    factor = jnp.minimum(1.0, 1.0 / jnp.sqrt(squares_all / param_count + 1e-06))
    updates = [member * factor for member in summed]
    return (latent_grad, updates[0], updates[1], updates[2], updates[3])


def solution(mesh):
    placed = (P("dp", None, "tm"), P("dp", "tm"), P(), P(), P(), P())
    return jax.shard_map(
        local,
        mesh=mesh,
        in_specs=placed,
        out_specs=(P("dp", None, "tm"), P(), P(), P(), P()),
        check_vma=False,
    )
```

profile of v0, /device:TPU:0, one launch (start us, length us, event | category | flops | bytes accessed | tf_op | source)
XLA Modules:
  0.0 188.2 jit_solution(7671481007626582187)
XLA Ops:
  0.6 1.3 slice.296
  1.9 1.3 collective-permute-start.3
  4.1 5.5 %collective-permute-start = (f32[1,64,4]{2,1,0:T(8,128)S(1)}, f32[1,64,4]{2,1,0:T(8,128)S(1)}, u32[]{:S(2)}, u32[]{:S(2)}) collective-permute-start(f32[1,64,4]{2,1,0:T(8,128)S(1)} %get-tuple-element.15), channel_id=1, source_target_pairs={{0,1},{1,2},{2,3},{3,4},{4,5},{5,6},{6,7},{8,9},{9,10},{10,11},{11... | collective-permute-start | bytes 3080 | tf_op jit(solution)/shard_map/ppermute | solution.py:20
  9.6 1.3 collective-permute-start.1
  12.3 1.6 slice_bitcast_fusion.6
  13.9 1.2 sine_multiply_fusion.1
  15.1 9.4 %sine_multiply_fusion = (f32[1024,512]{1,0:T(8,128)S(1)}, f32[1024,512]{1,0:T(8,128)}) fusion(f32[1024]{0:T(1024)S(1)} %fusion.218, f32[1024]{0:T(1024)S(1)} %multiply_subtract_fusion), kind=kLoop, calls=%fused_computation.21 | loop fusion | flops 8388608 | bytes 4202496 | tf_op jit(solution)/shard_map/jvp()/mul | solution.py:57
  25.3 1.1 compare_select_fusion
  26.7 1.2 copy.16
  28.1 1.0 fusion.69
  29.1 1.3 convolution_add_fusion.1
  30.4 1.0 fusion.5
  31.4 1.3 compare_select_fusion.9
  32.7 1.0 convolution_reduce_fusion.2
  33.7 1.0 convolution_reduce_fusion.1
  34.7 1.0 convolution_reduce_fusion
  35.7 1.0 convolution_reduce_fusion.5
  36.7 1.0 convolution_reduce_fusion.4
  37.6 1.0 convolution_reduce_fusion.6
  38.6 1.0 convolution_reduce_fusion.3
  39.6 2.0 %multiply_reduce_fusion.6 = (f32[]{:T(128)}, f32[1,1024]{1,0:T(1,128)}, f32[1,1792]{1,0:T(1,128)S(1)}) fusion(f32[1,1024]{1,0:T(1,128)} %param.8, f32[1,1040]{1,0:T(1,128)S(1)} %squeeze.11), kind=kLoop, calls=%fused_computation.340 | loop fusion | flops 4094 | bytes 16388 | tf_op jit(solution)/shard_map/reduce_sum | solution.py:220
  42.3 1.3 collective-permute-start.2
  45.4 1.3 reduce.11
  46.7 1.3 reshape.962
  48.0 1.4 reshape.970
  51.1 4.3 %fusion.15 = f32[1,4,1024]{2,1,0:T(4,128)} fusion(f32[1024,512]{1,0:T(8,128)S(1)} %get-tuple-element.77, f32[1024,512]{1,0:T(8,128)} %get-tuple-element.78, f32[1,4,256]{2,1,0:T(4,128)S(1)} %get-tuple-element.45, f32[1,4,256]{2,1,0:T(4,128)S(1)} %get-tuple-element.46, f32[1,4,256]{2,1,0:T(4,128)S(1)} %get-tuple-element.47, ...), kind=kOutput, calls=%fused_computation.33 | convolution fusion | flops 51392512 | bytes 4227072 | tf_op jit(solution)/shard_map/...nf,fk->...nk/dot_general | solution.py:36
  55.4 0.9 convolution_bitcast_fusion.10
  56.3 1.3 maximum_reduce_fusion
  57.6 1.3 reshape.959
  58.9 1.3 fusion.210
  60.2 1.4 reshape.967
  61.6 1.4 fusion.285
  63.0 0.9 fusion.283
  63.9 1.2 convolution_bitcast_fusion.11
  65.9 0.9 fusion.20
  67.6 1.3 convolution_bitcast_fusion.9
  69.7 1.4 reshape.974
  71.7 6.2 %collective-permute-start.5 = (f32[1,768]{1,0:T(1,128)S(1)}, f32[1,768]{1,0:T(1,128)S(1)}, u32[]{:S(2)}, u32[]{:S(2)}) collective-permute-start(f32[1,768]{1,0:T(1,128)S(1)} %pad.112), channel_id=1, source_target_pairs={{0,1},{1,2},{2,3},{3,4},{4,5},{5,6},{6,7},{8,9},{9,10},{10,11},{11... | collective-permute-start | bytes 9224 | tf_op jit(solution)/shard_map/ppermute | solution.py:32
  78.0 3.7 %fusion.14 = f32[1,4,1024]{2,1,0:T(4,128)S(1)} fusion(f32[1024,512]{1,0:T(8,128)S(1)} %get-tuple-element.77, f32[1024,512]{1,0:T(8,128)} %get-tuple-element.78, f32[1,4,256]{2,1,0:T(4,128)} %get-tuple-element.49, f32[1,4,256]{2,1,0:T(4,128)} %get-tuple-element.50, f32[1,4,256]{2,1,0:T(4,128)} %get-tuple-element.51, f32[1,4,256]{2,1,0:T(4,128)} %get-tuple-element.48), kind=kOutput, calls=%fused_computation.32 | convolution fusion | flops 51392512 | bytes 4227072 | tf_op jit(solution)/shard_map/jvp(...nf,fk->...nk)/dot_general | solution.py:36
  83.3 3.5 %fusion.16 = f32[1,4,1024]{2,1,0:T(4,128)S(1)} fusion(f32[1024,512]{1,0:T(8,128)S(1)} %get-tuple-element.77, f32[1024,512]{1,0:T(8,128)S(1)} %copy-done.1, f32[1,4,512]{2,1,0:T(4,128)S(1)} %get-tuple-element.18, f32[1,4,512]{2,1,0:T(4,128)S(1)} %get-tuple-element.17), kind=kOutput, calls=%fused_computation.34 | convolution fusion | flops 51384320 | bytes 4227072 | tf_op jit(solution)/shard_map/transpose(jvp(...nf,fk->...nk))/dot_general | solution.py:36
  86.9 5.0 %collective-permute-start.4 = (f32[1,768]{1,0:T(1,128)S(1)}, f32[1,768]{1,0:T(1,128)S(1)}, u32[]{:S(2)}, u32[]{:S(2)}) collective-permute-start(f32[1,768]{1,0:T(1,128)S(1)} %slice.347), channel_id=1, source_target_pairs={{0,1},{1,2},{2,3},{3,4},{4,5},{5,6},{6,7},{8,9},{9,10},{10,11},{11... | collective-permute-start | bytes 9224 | tf_op jit(solution)/shard_map/ppermute | solution.py:32
  93.8 2.0 %pad_maximum_fusion.16 = f32[1,3]{1,0:T(1,128)S(1)} fusion(f32[1,1]{1,0:T(1,128)} %bitcast.63, f32[1,1]{1,0:T(1,128)} %bitcast.53, f32[1,1]{1,0:T(1,128)} %bitcast.43), kind=kLoop, calls=%fused_computation.344 | loop fusion | flops 6 | bytes 24 | tf_op jit(solution)/shard_map/stack | solution.py:220
  96.0 22.0 %psum.35 = f32[1,3]{1,0:T(1,128)S(1)} all-reduce(f32[1,3]{1,0:T(1,128)S(1)} %pad_maximum_fusion.16), channel_id=1, replica_groups=mesh['dp'=4,'tm'=8] {'tm'}, use_global_device_ids=true, to_apply=%region_3.4 | all-reduce | flops 3 | bytes 24 | tf_op jit(solution)/shard_map/psum | solution.py:221
  119.8 2.1 %add_bitcast_fusion.1 = f32[1,1,1024]{2,1,0:T(1,128)S(1)} fusion(f32[1,1024]{1,0:T(1,128)S(1)} %get-tuple-element.14, f32[1,1024]{1,0:T(1,128)S(1)} %get-tuple-element.12, f32[]{:T(128)} %bitcast.66, f32[]{:T(128)} %bitcast.65, f32[]{:T(128)} %bitcast.64, f32[1,1024]{1,0:T(1,128)} %param.8, f32[1,1040]{1,0:T(1,128)} %copy-done.14), kind=kLoop, calls=%fused_computation.336 | loop fusion | flops 6144 | bytes 20492 | tf_op jit(solution)/shard_map/broadcast_in_dim | solution.py:226
  122.0 1.3 collective-permute-start.7
  123.3 4.5 %collective-permute-start.6 = (f32[1,1,8]{2,1,0:T(1,128)S(1)}, f32[1,1,8]{2,1,0:T(1,128)S(1)}, u32[]{:S(2)}, u32[]{:S(2)}) collective-permute-start(f32[1,1,8]{2,1,0:T(1,128)S(1)} %get-tuple-element.62), channel_id=1, source_target_pairs={{0,1},{1,2},{2,3},{3,4},{4,5},{5,6},{6,7},{8,9},{9,10},{10,11},{11... | collective-permute-start | bytes 104 | tf_op jit(solution)/shard_map/ppermute | solution.py:20
  127.8 1.3 collective-permute-done.6
  136.8 41.8 %all-reduce.29 = (f32[4,32,64]{2,1,0:T(8,128)S(1)}, f32[3,16,32]{2,1,0:T(8,128)S(1)}, f32[32,16]{0,1:T(8,128)S(1)}, f32[7,32]{1,0:T(8,128)S(1)}) all-reduce(f32[4,32,64]{2,1,0:T(8,128)S(1)} %maximum_bitcast_fusion, f32[3,16,32]{2,1,0:T(8,128)S(1)} %maximum_bitcast_fusion.1, ...), channel_id=1, replica_groups=mesh['dp'=4,'tm'=8] {'dp','tm'}, use_global_device_ids=true, to_apply=%region_4.5 | all-reduce | flops 10464 | bytes 83712 | tf_op jit(solution)/shard_map/psum | solution.py:256
  (141 shorter events, 30.2 us)
Async XLA Ops:
  0.6 30.8 %copy-start = (f32[32,16]{0,1:T(8,128)S(1)}, f32[32,16]{0,1:T(8,128)}, u32[]{:S(2)}) copy-start(f32[32,16]{0,1:T(8,128)} %param.11) | copy-start | bytes 6148
  1.9 41.6 %collective-permute-start.3 = (f32[1,768]{1,0:T(1,128)}, f32[1,768]{1,0:T(1,128)}, u32[]{:S(2)}, u32[]{:S(2)}) collective-permute-start(f32[1,768]{1,0:T(1,128)} %slice.296), channel_id=1, source_target_pairs={{1,0},{2,1},{3,2},{4,3},{5,4},{6,5},{7,6},{9,8},{10,9},{11,10},{12... | collective-permute-start | bytes 9224 | tf_op jit(solution)/shard_map/ppermute | solution.py:32
  4.1 20.5 %collective-permute-start = (f32[1,64,4]{2,1,0:T(8,128)S(1)}, f32[1,64,4]{2,1,0:T(8,128)S(1)}, u32[]{:S(2)}, u32[]{:S(2)}) collective-permute-start(f32[1,64,4]{2,1,0:T(8,128)S(1)} %get-tuple-element.15), channel_id=1, source_target_pairs={{0,1},{1,2},{2,3},{3,4},{4,5},{5,6},{6,7},{8,9},{9,10},{10,11},{11... | collective-permute-start | bytes 3080 | tf_op jit(solution)/shard_map/ppermute | solution.py:20
  9.6 15.0 %collective-permute-start.1 = (f32[1,64,4]{2,1,0:T(8,128)S(1)}, f32[1,64,4]{2,1,0:T(8,128)S(1)}, u32[]{:S(2)}, u32[]{:S(2)}) collective-permute-start(f32[1,64,4]{2,1,0:T(8,128)S(1)} %get-tuple-element.16), channel_id=1, source_target_pairs={{1,0},{2,1},{3,2},{4,3},{5,4},{6,5},{7,6},{9,8},{10,9},{11,10},{12... | collective-permute-start | bytes 3080 | tf_op jit(solution)/shard_map/ppermute | solution.py:22
  15.1 9.5 %copy-start.7 = (f32[1,64,512]{2,1,0:T(8,128)S(1)}, f32[1,64,512]{2,1,0:T(8,128)}, u32[]{:S(2)}) copy-start(f32[1,64,512]{2,1,0:T(8,128)} %param.7) | copy-start | bytes 393220
  15.1 9.5 %copy-start.11 = (f32[4,32,64]{2,1,0:T(8,128)S(1)}, f32[4,32,64]{2,1,0:T(8,128)}, u32[]{:S(2)}) copy-start(f32[4,32,64]{2,1,0:T(8,128)} %param.9) | copy-start | bytes 98308
  24.6 0.6 copy-start.17
  24.6 0.6 copy-start.19
  25.3 1.1 copy-start.4
  28.0 2.4 %copy-start.6 = (f32[1,32,1040]{2,1,0:T(8,128)}, f32[1,32,1040]{2,1,0:T(8,128)S(1)}, u32[]{:S(2)}) copy-start(f32[1,32,1040]{2,1,0:T(8,128)S(1)} %copy.17) | copy-start | bytes 399364
  32.7 5.9 %copy-start.9 = (f32[1,32,1040]{2,1,0:T(8,128)}, f32[1,32,1040]{2,1,0:T(8,128)S(1)}, u32[]{:S(2)}) copy-start(f32[1,32,1040]{2,1,0:T(8,128)S(1)} %get-tuple-element.74) | copy-start | bytes 399364
  39.6 2.0 %copy-start.14 = (f32[1,1040]{1,0:T(1,128)}, f32[1,1040]{1,0:T(1,128)S(1)}, u32[]{:S(2)}) copy-start(f32[1,1040]{1,0:T(1,128)S(1)} %squeeze.11) | copy-start | bytes 12484
  42.3 14.1 %collective-permute-start.2 = (f32[1,768]{1,0:T(1,128)}, f32[1,768]{1,0:T(1,128)}, u32[]{:S(2)}, u32[]{:S(2)}) collective-permute-start(f32[1,768]{1,0:T(1,128)} %slice.333), channel_id=1, source_target_pairs={{1,0},{2,1},{3,2},{4,3},{5,4},{6,5},{7,6},{9,8},{10,9},{11,10},{12... | collective-permute-start | bytes 9224 | tf_op jit(solution)/shard_map/ppermute | solution.py:32
  44.2 0.6 copy-start.15
  51.1 4.3 %copy-start.2 = (f32[256,128]{1,0:T(8,128)S(1)}, f32[256,128]{1,0:T(8,128)}, u32[]{:S(2)}) copy-start(f32[256,128]{1,0:T(8,128)} %get-tuple-element.75) | copy-start | bytes 393220
  51.1 4.3 %copy-start.3 = (f32[256,128]{1,0:T(8,128)S(1)}, f32[256,128]{1,0:T(8,128)}, u32[]{:S(2)}) copy-start(f32[256,128]{1,0:T(8,128)} %get-tuple-element.76) | copy-start | bytes 393220
  51.1 5.2 %copy-start.16 = (f32[1,1024]{1,0:T(1,128)S(1)}, f32[1,1024]{1,0:T(1,128)}, u32[]{:S(2)}) copy-start(f32[1,1024]{1,0:T(1,128)} %get-tuple-element.53) | copy-start | bytes 12292
  71.7 20.1 %collective-permute-start.5 = (f32[1,768]{1,0:T(1,128)S(1)}, f32[1,768]{1,0:T(1,128)S(1)}, u32[]{:S(2)}, u32[]{:S(2)}) collective-permute-start(f32[1,768]{1,0:T(1,128)S(1)} %pad.112), channel_id=1, source_target_pairs={{0,1},{1,2},{2,3},{3,4},{4,5},{5,6},{6,7},{8,9},{9,10},{10,11},{11... | collective-permute-start | bytes 9224 | tf_op jit(solution)/shard_map/ppermute | solution.py:32
  78.0 3.7 %copy-start.23 = (f32[64]{0:T(128)S(1)}, f32[64]{0:T(128)}, u32[]{:S(2)}) copy-start(f32[64]{0:T(128)} %get-tuple-element.67) | copy-start | bytes 772
  78.0 3.7 %copy-start.24 = (f32[64]{0:T(128)S(1)}, f32[64]{0:T(128)}, u32[]{:S(2)}) copy-start(f32[64]{0:T(128)} %get-tuple-element.68) | copy-start | bytes 772
  78.0 4.1 %copy-start.22 = (f32[1,4,1024]{2,1,0:T(4,128)S(1)}, f32[1,4,1024]{2,1,0:T(4,128)}, u32[]{:S(2)}) copy-start(f32[1,4,1024]{2,1,0:T(4,128)} %fusion.15) | copy-start | bytes 49156
  81.7 1.6 copy-start.1
  83.3 8.6 %copy-start.21 = (f32[1,1216]{1,0:T(1,128)S(1)}, f32[1,1216]{1,0:T(1,128)}, u32[]{:S(2)}) copy-start(f32[1,1216]{1,0:T(1,128)} %reshape.974) | copy-start | bytes 14596
  86.8 43.6 %copy-start.10 = (f32[1,32,1040]{2,1,0:T(8,128)S(1)}, f32[1,32,1040]{2,1,0:T(8,128)}, u32[]{:S(2)}) copy-start(f32[1,32,1040]{2,1,0:T(8,128)} %copy-done.9) | copy-start | bytes 399364
  86.9 6.3 %collective-permute-start.4 = (f32[1,768]{1,0:T(1,128)S(1)}, f32[1,768]{1,0:T(1,128)S(1)}, u32[]{:S(2)}, u32[]{:S(2)}) collective-permute-start(f32[1,768]{1,0:T(1,128)S(1)} %slice.347), channel_id=1, source_target_pairs={{0,1},{1,2},{2,3},{3,4},{4,5},{5,6},{6,7},{8,9},{9,10},{10,11},{11... | collective-permute-start | bytes 9224 | tf_op jit(solution)/shard_map/ppermute | solution.py:32
  122.0 5.8 %collective-permute-start.7 = (f32[1,1,8]{2,1,0:T(1,128)S(1)}, f32[1,1,8]{2,1,0:T(1,128)S(1)}, u32[]{:S(2)}, u32[]{:S(2)}) collective-permute-start(f32[1,1,8]{2,1,0:T(1,128)S(1)} %get-tuple-element.61), channel_id=1, source_target_pairs={{1,0},{2,1},{3,2},{4,3},{5,4},{6,5},{7,6},{9,8},{10,9},{11,10},{12... | collective-permute-start | bytes 104 | tf_op jit(solution)/shard_map/ppermute | solution.py:22
  123.3 5.8 %collective-permute-start.6 = (f32[1,1,8]{2,1,0:T(1,128)S(1)}, f32[1,1,8]{2,1,0:T(1,128)S(1)}, u32[]{:S(2)}, u32[]{:S(2)}) collective-permute-start(f32[1,1,8]{2,1,0:T(1,128)S(1)} %get-tuple-element.62), channel_id=1, source_target_pairs={{0,1},{1,2},{2,3},{3,4},{4,5},{5,6},{6,7},{8,9},{9,10},{10,11},{11... | collective-permute-start | bytes 104 | tf_op jit(solution)/shard_map/ppermute | solution.py:20
  129.2 3.1 %copy-start.13 = (f32[3,16,32]{2,1,0:T(8,128)S(1)}, f32[3,16,32]{2,1,0:T(8,128)}, u32[]{:S(2)}) copy-start(f32[3,16,32]{2,1,0:T(8,128)} %param.10) | copy-start | bytes 18436
  131.2 2.7 %copy-start.5 = (f32[1,64,519]{2,1,0:T(8,128)S(1)}, f32[1,64,519]{2,1,0:T(8,128)}, u32[]{:S(2)}) copy-start(f32[1,64,519]{2,1,0:T(8,128)} %copy-done.4) | copy-start | bytes 398596
  131.7 2.7 %copy-start.8 = (f32[1,64,512]{2,1,0:T(8,128)S(1)}, f32[1,64,512]{2,1,0:T(8,128)}, u32[]{:S(2)}) copy-start(f32[1,64,512]{2,1,0:T(8,128)} %param.7) | copy-start | bytes 393220
  131.7 2.7 %copy-start.18 = (f32[1,64,4]{2,1,0:T(8,128)S(1)}, f32[1,64,4]{2,1,0:T(8,128)}, u32[]{:S(2)}) copy-start(f32[1,64,4]{2,1,0:T(8,128)} %copy-done.17) | copy-start | bytes 3076
  131.7 2.7 %copy-start.20 = (f32[1,64,4]{2,1,0:T(8,128)S(1)}, f32[1,64,4]{2,1,0:T(8,128)}, u32[]{:S(2)}) copy-start(f32[1,64,4]{2,1,0:T(8,128)} %copy-done.19) | copy-start | bytes 3076
  134.0 52.6 %copy-start.12 = (f32[4,32,64]{2,1,0:T(8,128)S(1)}, f32[4,32,64]{2,1,0:T(8,128)}, u32[]{:S(2)}) copy-start(f32[4,32,64]{2,1,0:T(8,128)} %param.9) | copy-start | bytes 98308
where the time goes:
time: 190 us; the launch traced here: 188 us
  blocking collectives  63.8 us (34%)
  matrix products  37.6 us (20%)
  other arithmetic  31.8 us (17%)
  starting transfers between devices  26.4 us (14%)
  local copies, waits for them, and re-layouts  22 us (12%)
  between operations  4.65 us (2%)
  waiting for transfers between devices  1.95 us (1%)
    psum x1, blocking collectives, local(): lax.psum((local_totals[0], local_totals[1], local_totals[2], local_totals...  41.8 us
    dot_general x44, matrix products, product(): jnp.einsum(form, left, right, precision=lax.Precision.HIGHEST, preferred_...  37.6 us
    psum x1, blocking collectives, local(): squares = lax.psum(squares, 'tm')  22 us
    ppermute x4, starting transfers between devices, from_behind(): return lax.ppermute(x, axis, pairs)  13.8 us
    mul x2, other arithmetic, dft_table(): -hann_taper * jnp.sin(angles)  10.7 us
    ppermute x2, starting transfers between devices, padded_2(): lax.ppermute(tail, axis, [(i, (i + 1) % count) for i in range(ends)])  10.1 us
    reshape x5, local copies, waits for them, and re-layouts, framed(): blocks = signal.reshape(signal.shape[:-1] + (frame_count + 3, hop_size))  6.68 us
    slice x4, local copies, waits for them, and re-layouts, framed(): blocks[..., offset:offset + frame_count, :]  4.01 us
  transfers between devices with their start and end apart: 8, of which 2 were waited for; matrix products, arithmetic and copies ran while one was open for 28% of the time, Pallas kernels for 0%

commit v1 on v0

--- a/solution.py
+++ b/solution.py
@@ -254,7 +254,7 @@
     ]
     param_count = sum((member.size for member in local_totals))
     summed = lax.psum(
-        (local_totals[0], local_totals[1], local_totals[2], local_totals[3]), ("dp", "tm")
+        lax.psum((local_totals[0], local_totals[1], local_totals[2], local_totals[3]), "dp"), "tm"
     )
     squares_all = sum((jnp.sum(member * member) for member in summed))
     factor = jnp.minimum(1.0, 1.0 / jnp.sqrt(squares_all / param_count + 1e-06))

time: 190 us -> 196 us (1.032)
  blocking collectives: 63.8 us -> 69.8 us
    psum x0 -> x1, blocking collectives: none -> 36.5 us  [local(): lax.psum(lax.psum((local_totals[0], local_totals[1], local_totals[2], loc...]
    psum x1, blocking collectives: 41.8 us -> 11.3 us  [local(): lax.psum((local_totals[0], local_totals[1], local_totals[2], local_totals...]
  transfers between devices with their start and end apart: 8 -> 8, of which waited for: 2 -> 2; matrix products, arithmetic and copies ran while one was open for 28% -> 27% of each run, Pallas kernels for 0% -> 0%
where the time goes in v1:
time: 196 us; the launch traced here: 194 us
  blocking collectives  69.8 us (36%)
  matrix products  37.6 us (19%)
  other arithmetic  31.8 us (16%)
  starting transfers between devices  26.4 us (13%)
  local copies, waits for them, and re-layouts  21.8 us (11%)
  between operations  4.69 us (2%)
    dot_general x44, matrix products, product(): jnp.einsum(form, left, right, precision=lax.Precision.HIGHEST, preferred_...  37.6 us
    psum x1, blocking collectives, local(): lax.psum(lax.psum((local_totals[0], local_totals[1], local_totals[2], loc...  36.5 us
    psum x1, blocking collectives, local(): squares = lax.psum(squares, 'tm')  22 us
    ppermute x4, starting transfers between devices, from_behind(): return lax.ppermute(x, axis, pairs)  13.8 us
    psum x1, blocking collectives, local(): lax.psum((local_totals[0], local_totals[1], local_totals[2], local_totals...  11.3 us
    mul x2, other arithmetic, dft_table(): -hann_taper * jnp.sin(angles)  10.7 us
    ppermute x2, starting transfers between devices, padded_2(): lax.ppermute(tail, axis, [(i, (i + 1) % count) for i in range(ends)])  10.1 us
    reshape x5, local copies, waits for them, and re-layouts, framed(): blocks = signal.reshape(signal.shape[:-1] + (frame_count + 3, hop_size))  6.68 us
  transfers between devices with their start and end apart: 8, of which 2 were waited for; matrix products, arithmetic and copies ran while one was open for 27% of the time, Pallas kernels for 0%

profile of v1, /device:TPU:0, one launch (start us, length us, event | category | flops | bytes accessed | tf_op | source)
XLA Modules:
  0.0 194.1 jit_solution(8169802335826273108)
XLA Ops:
  0.6 1.3 slice.296
  1.9 1.3 collective-permute-start.3
  4.1 5.5 %collective-permute-start = (f32[1,64,4]{2,1,0:T(8,128)S(1)}, f32[1,64,4]{2,1,0:T(8,128)S(1)}, u32[]{:S(2)}, u32[]{:S(2)}) collective-permute-start(f32[1,64,4]{2,1,0:T(8,128)S(1)} %get-tuple-element.19), channel_id=1, source_target_pairs={{0,1},{1,2},{2,3},{3,4},{4,5},{5,6},{6,7},{8,9},{9,10},{10,11},{11... | collective-permute-start | bytes 3080 | tf_op jit(solution)/shard_map/ppermute | solution.py:20
  9.6 1.3 collective-permute-start.1
  12.3 1.6 slice_bitcast_fusion.6
  13.9 1.2 sine_multiply_fusion.1
  15.1 9.4 %sine_multiply_fusion = (f32[1024,512]{1,0:T(8,128)S(1)}, f32[1024,512]{1,0:T(8,128)}) fusion(f32[1024]{0:T(1024)S(1)} %fusion.218, f32[1024]{0:T(1024)S(1)} %multiply_subtract_fusion), kind=kLoop, calls=%fused_computation.21 | loop fusion | flops 8388608 | bytes 4202496 | tf_op jit(solution)/shard_map/jvp()/mul | solution.py:57
  25.2 1.1 compare_select_fusion
  26.5 1.2 copy.16
  28.0 1.0 fusion.69
  29.0 1.3 convolution_add_fusion.1
  30.3 1.0 fusion.5
  31.3 1.3 compare_select_fusion.9
  32.6 1.0 convolution_reduce_fusion.2
  33.6 1.0 convolution_reduce_fusion.1
  34.6 1.0 convolution_reduce_fusion
  35.5 1.0 convolution_reduce_fusion.5
  36.5 1.0 convolution_reduce_fusion.4
  37.5 1.0 convolution_reduce_fusion.6
  38.5 1.0 convolution_reduce_fusion.3
  39.5 2.0 %multiply_reduce_fusion.6 = (f32[]{:T(128)}, f32[1,1024]{1,0:T(1,128)}, f32[1,1792]{1,0:T(1,128)S(1)}) fusion(f32[1,1024]{1,0:T(1,128)} %param.8, f32[1,1040]{1,0:T(1,128)S(1)} %squeeze.11), kind=kLoop, calls=%fused_computation.340 | loop fusion | flops 4094 | bytes 16388 | tf_op jit(solution)/shard_map/reduce_sum | solution.py:220
  42.1 1.3 collective-permute-start.2
  45.3 1.3 reduce.11
  46.6 1.3 reshape.962
  47.9 1.4 reshape.970
  51.0 4.3 %fusion.15 = f32[1,4,1024]{2,1,0:T(4,128)} fusion(f32[1024,512]{1,0:T(8,128)S(1)} %get-tuple-element.81, f32[1024,512]{1,0:T(8,128)} %get-tuple-element.82, f32[1,4,256]{2,1,0:T(4,128)S(1)} %get-tuple-element.49, f32[1,4,256]{2,1,0:T(4,128)S(1)} %get-tuple-element.50, f32[1,4,256]{2,1,0:T(4,128)S(1)} %get-tuple-element.51, ...), kind=kOutput, calls=%fused_computation.33 | convolution fusion | flops 51392512 | bytes 4227072 | tf_op jit(solution)/shard_map/...nf,fk->...nk/dot_general | solution.py:36
  55.3 0.9 convolution_bitcast_fusion.10
  56.2 1.3 maximum_reduce_fusion
  57.5 1.3 reshape.959
  58.8 1.3 fusion.210
  60.1 1.4 reshape.967
  61.4 1.4 fusion.285
  63.7 1.2 convolution_bitcast_fusion.11
  65.8 0.9 fusion.20
  67.5 1.3 convolution_bitcast_fusion.9
  69.5 1.4 reshape.974
  71.6 6.3 %collective-permute-start.5 = (f32[1,768]{1,0:T(1,128)S(1)}, f32[1,768]{1,0:T(1,128)S(1)}, u32[]{:S(2)}, u32[]{:S(2)}) collective-permute-start(f32[1,768]{1,0:T(1,128)S(1)} %pad.112), channel_id=1, source_target_pairs={{0,1},{1,2},{2,3},{3,4},{4,5},{5,6},{6,7},{8,9},{9,10},{10,11},{11... | collective-permute-start | bytes 9224 | tf_op jit(solution)/shard_map/ppermute | solution.py:32
  77.9 3.7 %fusion.14 = f32[1,4,1024]{2,1,0:T(4,128)S(1)} fusion(f32[1024,512]{1,0:T(8,128)S(1)} %get-tuple-element.81, f32[1024,512]{1,0:T(8,128)} %get-tuple-element.82, f32[1,4,256]{2,1,0:T(4,128)} %get-tuple-element.53, f32[1,4,256]{2,1,0:T(4,128)} %get-tuple-element.54, f32[1,4,256]{2,1,0:T(4,128)} %get-tuple-element.55, f32[1,4,256]{2,1,0:T(4,128)} %get-tuple-element.52), kind=kOutput, calls=%fused_computation.32 | convolution fusion | flops 51392512 | bytes 4227072 | tf_op jit(solution)/shard_map/jvp(...nf,fk->...nk)/dot_general | solution.py:36
  83.2 3.5 %fusion.16 = f32[1,4,1024]{2,1,0:T(4,128)S(1)} fusion(f32[1024,512]{1,0:T(8,128)S(1)} %get-tuple-element.81, f32[1024,512]{1,0:T(8,128)S(1)} %copy-done.1, f32[1,4,512]{2,1,0:T(4,128)S(1)} %get-tuple-element.22, f32[1,4,512]{2,1,0:T(4,128)S(1)} %get-tuple-element.21), kind=kOutput, calls=%fused_computation.34 | convolution fusion | flops 51384320 | bytes 4227072 | tf_op jit(solution)/shard_map/transpose(jvp(...nf,fk->...nk))/dot_general | solution.py:36
  86.8 5.0 %collective-permute-start.4 = (f32[1,768]{1,0:T(1,128)S(1)}, f32[1,768]{1,0:T(1,128)S(1)}, u32[]{:S(2)}, u32[]{:S(2)}) collective-permute-start(f32[1,768]{1,0:T(1,128)S(1)} %slice.347), channel_id=1, source_target_pairs={{0,1},{1,2},{2,3},{3,4},{4,5},{5,6},{6,7},{8,9},{9,10},{10,11},{11... | collective-permute-start | bytes 9224 | tf_op jit(solution)/shard_map/ppermute | solution.py:32
  93.7 2.0 %pad_maximum_fusion.16 = f32[1,3]{1,0:T(1,128)S(1)} fusion(f32[1,1]{1,0:T(1,128)} %bitcast.63, f32[1,1]{1,0:T(1,128)} %bitcast.53, f32[1,1]{1,0:T(1,128)} %bitcast.43), kind=kLoop, calls=%fused_computation.344 | loop fusion | flops 6 | bytes 24 | tf_op jit(solution)/shard_map/stack | solution.py:220
  95.8 22.0 %psum.63 = f32[1,3]{1,0:T(1,128)S(1)} all-reduce(f32[1,3]{1,0:T(1,128)S(1)} %pad_maximum_fusion.16), channel_id=1, replica_groups=mesh['dp'=4,'tm'=8] {'tm'}, use_global_device_ids=true, to_apply=%region_3.4 | all-reduce | flops 3 | bytes 24 | tf_op jit(solution)/shard_map/psum | solution.py:221
  119.7 2.1 %add_bitcast_fusion.1 = f32[1,1,1024]{2,1,0:T(1,128)S(1)} fusion(f32[1,1024]{1,0:T(1,128)S(1)} %get-tuple-element.18, f32[1,1024]{1,0:T(1,128)S(1)} %get-tuple-element.16, f32[]{:T(128)} %bitcast.66, f32[]{:T(128)} %bitcast.65, f32[]{:T(128)} %bitcast.64, f32[1,1024]{1,0:T(1,128)} %param.8, f32[1,1040]{1,0:T(1,128)} %copy-done.14), kind=kLoop, calls=%fused_computation.336 | loop fusion | flops 6144 | bytes 20492 | tf_op jit(solution)/shard_map/broadcast_in_dim | solution.py:226
  121.9 1.3 collective-permute-start.7
  123.2 4.5 %collective-permute-start.6 = (f32[1,1,8]{2,1,0:T(1,128)S(1)}, f32[1,1,8]{2,1,0:T(1,128)S(1)}, u32[]{:S(2)}, u32[]{:S(2)}) collective-permute-start(f32[1,1,8]{2,1,0:T(1,128)S(1)} %get-tuple-element.66), channel_id=1, source_target_pairs={{0,1},{1,2},{2,3},{3,4},{4,5},{5,6},{6,7},{8,9},{9,10},{10,11},{11... | collective-permute-start | bytes 104 | tf_op jit(solution)/shard_map/ppermute | solution.py:20
  127.7 1.3 collective-permute-done.6
  136.7 11.3 %all-reduce.30 = (f32[4,32,64]{2,1,0:T(8,128)S(1)}, f32[3,16,32]{2,1,0:T(8,128)S(1)}, f32[32,16]{0,1:T(8,128)S(1)}, f32[7,32]{1,0:T(8,128)S(1)}) all-reduce(f32[4,32,64]{2,1,0:T(8,128)S(1)} %maximum_bitcast_fusion, f32[3,16,32]{2,1,0:T(8,128)S(1)} %maximum_bitcast_fusion.1, ...), channel_id=1, replica_groups=mesh['dp'=4,'tm'=8] {'dp'}, use_global_device_ids=true, to_apply=%region_4.5 | all-reduce | flops 10464 | bytes 83712 | tf_op jit(solution)/shard_map/psum | solution.py:257
  148.0 36.5 %all-reduce.29 = (f32[4,32,64]{2,1,0:T(8,128)S(1)}, f32[3,16,32]{2,1,0:T(8,128)S(1)}, f32[32,16]{0,1:T(8,128)S(1)}, f32[7,32]{1,0:T(8,128)S(1)}) all-reduce(f32[4,32,64]{2,1,0:T(8,128)S(1)} %get-tuple-element.9, f32[3,16,32]{2,1,0:T(8,128)S(1)} %get-tuple-element.10, ...), channel_id=1, replica_groups=mesh['dp'=4,'tm'=8] {'tm'}, use_global_device_ids=true, to_apply=%region_5.6 | all-reduce | flops 10464 | bytes 83712 | tf_op jit(solution)/shard_map/psum | solution.py:256
  (142 shorter events, 31.0 us)
Async XLA Ops:
  0.6 30.6 %copy-start = (f32[32,16]{0,1:T(8,128)S(1)}, f32[32,16]{0,1:T(8,128)}, u32[]{:S(2)}) copy-start(f32[32,16]{0,1:T(8,128)} %param.11) | copy-start | bytes 6148
  1.9 41.5 %collective-permute-start.3 = (f32[1,768]{1,0:T(1,128)}, f32[1,768]{1,0:T(1,128)}, u32[]{:S(2)}, u32[]{:S(2)}) collective-permute-start(f32[1,768]{1,0:T(1,128)} %slice.296), channel_id=1, source_target_pairs={{1,0},{2,1},{3,2},{4,3},{5,4},{6,5},{7,6},{9,8},{10,9},{11,10},{12... | collective-permute-start | bytes 9224 | tf_op jit(solution)/shard_map/ppermute | solution.py:32
  4.1 20.5 %collective-permute-start = (f32[1,64,4]{2,1,0:T(8,128)S(1)}, f32[1,64,4]{2,1,0:T(8,128)S(1)}, u32[]{:S(2)}, u32[]{:S(2)}) collective-permute-start(f32[1,64,4]{2,1,0:T(8,128)S(1)} %get-tuple-element.19), channel_id=1, source_target_pairs={{0,1},{1,2},{2,3},{3,4},{4,5},{5,6},{6,7},{8,9},{9,10},{10,11},{11... | collective-permute-start | bytes 3080 | tf_op jit(solution)/shard_map/ppermute | solution.py:20
  9.6 15.0 %collective-permute-start.1 = (f32[1,64,4]{2,1,0:T(8,128)S(1)}, f32[1,64,4]{2,1,0:T(8,128)S(1)}, u32[]{:S(2)}, u32[]{:S(2)}) collective-permute-start(f32[1,64,4]{2,1,0:T(8,128)S(1)} %get-tuple-element.20), channel_id=1, source_target_pairs={{1,0},{2,1},{3,2},{4,3},{5,4},{6,5},{7,6},{9,8},{10,9},{11,10},{12... | collective-permute-start | bytes 3080 | tf_op jit(solution)/shard_map/ppermute | solution.py:22
  15.1 9.5 %copy-start.7 = (f32[1,64,512]{2,1,0:T(8,128)S(1)}, f32[1,64,512]{2,1,0:T(8,128)}, u32[]{:S(2)}) copy-start(f32[1,64,512]{2,1,0:T(8,128)} %param.7) | copy-start | bytes 393220
  15.1 9.5 %copy-start.11 = (f32[4,32,64]{2,1,0:T(8,128)S(1)}, f32[4,32,64]{2,1,0:T(8,128)}, u32[]{:S(2)}) copy-start(f32[4,32,64]{2,1,0:T(8,128)} %param.9) | copy-start | bytes 98308
  24.6 2.0 %copy-start.17 = (f32[1,64,4]{2,1,0:T(8,128)}, f32[1,64,4]{2,1,0:T(8,128)S(1)}, u32[]{:S(2)}) copy-start(f32[1,64,4]{2,1,0:T(8,128)S(1)} %collective-permute-done) | copy-start | bytes 3076
  24.6 1.9 %copy-start.19 = (f32[1,64,4]{2,1,0:T(8,128)}, f32[1,64,4]{2,1,0:T(8,128)S(1)}, u32[]{:S(2)}) copy-start(f32[1,64,4]{2,1,0:T(8,128)S(1)} %collective-permute-done.1) | copy-start | bytes 3076
  25.2 1.1 copy-start.4
  27.9 2.4 %copy-start.6 = (f32[1,32,1040]{2,1,0:T(8,128)}, f32[1,32,1040]{2,1,0:T(8,128)S(1)}, u32[]{:S(2)}) copy-start(f32[1,32,1040]{2,1,0:T(8,128)S(1)} %copy.17) | copy-start | bytes 399364
  32.6 5.9 %copy-start.9 = (f32[1,32,1040]{2,1,0:T(8,128)}, f32[1,32,1040]{2,1,0:T(8,128)S(1)}, u32[]{:S(2)}) copy-start(f32[1,32,1040]{2,1,0:T(8,128)S(1)} %get-tuple-element.78) | copy-start | bytes 399364
  39.5 2.0 %copy-start.14 = (f32[1,1040]{1,0:T(1,128)}, f32[1,1040]{1,0:T(1,128)S(1)}, u32[]{:S(2)}) copy-start(f32[1,1040]{1,0:T(1,128)S(1)} %squeeze.11) | copy-start | bytes 12484
  42.1 14.1 %collective-permute-start.2 = (f32[1,768]{1,0:T(1,128)}, f32[1,768]{1,0:T(1,128)}, u32[]{:S(2)}, u32[]{:S(2)}) collective-permute-start(f32[1,768]{1,0:T(1,128)} %slice.333), channel_id=1, source_target_pairs={{1,0},{2,1},{3,2},{4,3},{5,4},{6,5},{7,6},{9,8},{10,9},{11,10},{12... | collective-permute-start | bytes 9224 | tf_op jit(solution)/shard_map/ppermute | solution.py:32
  44.1 0.6 copy-start.15
  51.0 4.3 %copy-start.2 = (f32[256,128]{1,0:T(8,128)S(1)}, f32[256,128]{1,0:T(8,128)}, u32[]{:S(2)}) copy-start(f32[256,128]{1,0:T(8,128)} %get-tuple-element.79) | copy-start | bytes 393220
  51.0 4.3 %copy-start.3 = (f32[256,128]{1,0:T(8,128)S(1)}, f32[256,128]{1,0:T(8,128)}, u32[]{:S(2)}) copy-start(f32[256,128]{1,0:T(8,128)} %get-tuple-element.80) | copy-start | bytes 393220
  51.0 5.2 %copy-start.16 = (f32[1,1024]{1,0:T(1,128)S(1)}, f32[1,1024]{1,0:T(1,128)}, u32[]{:S(2)}) copy-start(f32[1,1024]{1,0:T(1,128)} %get-tuple-element.57) | copy-start | bytes 12292
  71.6 20.2 %collective-permute-start.5 = (f32[1,768]{1,0:T(1,128)S(1)}, f32[1,768]{1,0:T(1,128)S(1)}, u32[]{:S(2)}, u32[]{:S(2)}) collective-permute-start(f32[1,768]{1,0:T(1,128)S(1)} %pad.112), channel_id=1, source_target_pairs={{0,1},{1,2},{2,3},{3,4},{4,5},{5,6},{6,7},{8,9},{9,10},{10,11},{11... | collective-permute-start | bytes 9224 | tf_op jit(solution)/shard_map/ppermute | solution.py:32
  77.8 3.7 %copy-start.23 = (f32[64]{0:T(128)S(1)}, f32[64]{0:T(128)}, u32[]{:S(2)}) copy-start(f32[64]{0:T(128)} %get-tuple-element.71) | copy-start | bytes 772
  77.9 3.7 %copy-start.24 = (f32[64]{0:T(128)S(1)}, f32[64]{0:T(128)}, u32[]{:S(2)}) copy-start(f32[64]{0:T(128)} %get-tuple-element.72) | copy-start | bytes 772
  77.9 4.1 %copy-start.22 = (f32[1,4,1024]{2,1,0:T(4,128)S(1)}, f32[1,4,1024]{2,1,0:T(4,128)}, u32[]{:S(2)}) copy-start(f32[1,4,1024]{2,1,0:T(4,128)} %fusion.15) | copy-start | bytes 49156
  81.6 1.6 copy-start.1
  83.2 8.6 %copy-start.21 = (f32[1,1216]{1,0:T(1,128)S(1)}, f32[1,1216]{1,0:T(1,128)}, u32[]{:S(2)}) copy-start(f32[1,1216]{1,0:T(1,128)} %reshape.974) | copy-start | bytes 14596
  86.7 43.6 %copy-start.10 = (f32[1,32,1040]{2,1,0:T(8,128)S(1)}, f32[1,32,1040]{2,1,0:T(8,128)}, u32[]{:S(2)}) copy-start(f32[1,32,1040]{2,1,0:T(8,128)} %copy-done.9) | copy-start | bytes 399364
  86.8 6.3 %collective-permute-start.4 = (f32[1,768]{1,0:T(1,128)S(1)}, f32[1,768]{1,0:T(1,128)S(1)}, u32[]{:S(2)}, u32[]{:S(2)}) collective-permute-start(f32[1,768]{1,0:T(1,128)S(1)} %slice.347), channel_id=1, source_target_pairs={{0,1},{1,2},{2,3},{3,4},{4,5},{5,6},{6,7},{8,9},{9,10},{10,11},{11... | collective-permute-start | bytes 9224 | tf_op jit(solution)/shard_map/ppermute | solution.py:32
  121.9 5.8 %collective-permute-start.7 = (f32[1,1,8]{2,1,0:T(1,128)S(1)}, f32[1,1,8]{2,1,0:T(1,128)S(1)}, u32[]{:S(2)}, u32[]{:S(2)}) collective-permute-start(f32[1,1,8]{2,1,0:T(1,128)S(1)} %get-tuple-element.65), channel_id=1, source_target_pairs={{1,0},{2,1},{3,2},{4,3},{5,4},{6,5},{7,6},{9,8},{10,9},{11,10},{12... | collective-permute-start | bytes 104 | tf_op jit(solution)/shard_map/ppermute | solution.py:22
  123.2 5.8 %collective-permute-start.6 = (f32[1,1,8]{2,1,0:T(1,128)S(1)}, f32[1,1,8]{2,1,0:T(1,128)S(1)}, u32[]{:S(2)}, u32[]{:S(2)}) collective-permute-start(f32[1,1,8]{2,1,0:T(1,128)S(1)} %get-tuple-element.66), channel_id=1, source_target_pairs={{0,1},{1,2},{2,3},{3,4},{4,5},{5,6},{6,7},{8,9},{9,10},{10,11},{11... | collective-permute-start | bytes 104 | tf_op jit(solution)/shard_map/ppermute | solution.py:20
  129.1 3.1 %copy-start.13 = (f32[3,16,32]{2,1,0:T(8,128)S(1)}, f32[3,16,32]{2,1,0:T(8,128)}, u32[]{:S(2)}) copy-start(f32[3,16,32]{2,1,0:T(8,128)} %param.10) | copy-start | bytes 18436
  131.1 2.8 %copy-start.5 = (f32[1,64,519]{2,1,0:T(8,128)S(1)}, f32[1,64,519]{2,1,0:T(8,128)}, u32[]{:S(2)}) copy-start(f32[1,64,519]{2,1,0:T(8,128)} %copy-done.4) | copy-start | bytes 398596
  131.5 2.7 %copy-start.8 = (f32[1,64,512]{2,1,0:T(8,128)S(1)}, f32[1,64,512]{2,1,0:T(8,128)}, u32[]{:S(2)}) copy-start(f32[1,64,512]{2,1,0:T(8,128)} %param.7) | copy-start | bytes 393220
  131.5 2.7 %copy-start.18 = (f32[1,64,4]{2,1,0:T(8,128)S(1)}, f32[1,64,4]{2,1,0:T(8,128)}, u32[]{:S(2)}) copy-start(f32[1,64,4]{2,1,0:T(8,128)} %copy-done.17) | copy-start | bytes 3076
  131.5 2.7 %copy-start.20 = (f32[1,64,4]{2,1,0:T(8,128)S(1)}, f32[1,64,4]{2,1,0:T(8,128)}, u32[]{:S(2)}) copy-start(f32[1,64,4]{2,1,0:T(8,128)} %copy-done.19) | copy-start | bytes 3076
  133.8 58.7 %copy-start.12 = (f32[4,32,64]{2,1,0:T(8,128)S(1)}, f32[4,32,64]{2,1,0:T(8,128)}, u32[]{:S(2)}) copy-start(f32[4,32,64]{2,1,0:T(8,128)} %param.9) | copy-start | bytes 98308
